TPU v7x, 32 devices: a whole 2x2x4 slice. The times are simulated.
32 devices in a mesh: enc: 4 (over z), dp: 8 (over y, x, core).
Axes of the slice: x: 2, y: 2, z: 4, core: 2. Of those that a mesh axis runs over, the one named last changes fastest.
Arguments:
- text: bfloat16 [16384, 768], P(('enc', 'dp')), may hold values from -6 to 6
- region_feats: bfloat16 [13312, 2048], P(('enc', 'dp')), may hold values from -6 to 6
- boxes: bfloat16 [4, 13312], P(None, ('enc', 'dp')), may hold values from 0 to 1
- caption_count: int32 [128], P(('enc', 'dp')), may hold values from 8 to 128, as said below
- region_count: int32 [128], P(('enc', 'dp')), may hold values from 36 to 100, as said below
- region_offset: int32 [32], P(('enc', 'dp')), may hold values from 0 to 31
- w_img: bfloat16 [2048, 768], P(('enc', 'dp')), may hold values from -0.125 to 0.125
- w_box: bfloat16 [4, 768], replicated, may hold values from -3 to 3
- b_img: float32 [768], replicated, may hold values from -3 to 3
- g_reg: float32 [768], replicated, may hold values from 0.25 to 1.75
- beta_reg: float32 [768], replicated, may hold values from -1.75 to 1.75
- w_query: bfloat16 [768, 768], P(('enc', 'dp')), may hold values from -0.21875 to 0.21875
- b_query: float32 [768], replicated, may hold values from -1.75 to 1.75
- w_key: bfloat16 [768, 768], P(('enc', 'dp')), may hold values from -0.21875 to 0.21875
- w_value: bfloat16 [768, 768], P(('enc', 'dp')), may hold values from -0.21875 to 0.21875
- b_value: float32 [768], replicated, may hold values from -1.75 to 1.75
- w_out: bfloat16 [768, 768], P(('enc', 'dp')), may hold values from -1.75 to 1.75
- b_out: float32 [768], replicated, may hold values from -1.75 to 1.75
- g_one: float32 [768], replicated, may hold values from 0.25 to 1.75
- beta_one: float32 [768], replicated, may hold values from -1.75 to 1.75
- w_up: bfloat16 [768, 3072], P(('enc', 'dp')), may hold values from -0.21875 to 0.21875
- b_up: float32 [3072], replicated, may hold values from -1.75 to 1.75
- w_down: bfloat16 [3072, 768], P(('enc', 'dp')), may hold values from -0.109375 to 0.109375
- b_down: float32 [768], replicated, may hold values from -1.75 to 1.75
- g_two: float32 [768], replicated, may hold values from 0.25 to 1.75
- beta_two: float32 [768], replicated, may hold values from -1.75 to 1.75
- cotangent: bfloat16 [32768, 768], P(('enc', 'dp'))
Outputs:
- output: bfloat16 [32768, 768], P(('enc', 'dp'))
- grad_text: bfloat16 [16384, 768], P(('enc', 'dp'))
- grad_feats: bfloat16 [13312, 2048], P(('enc', 'dp'))
- grad_boxes: bfloat16 [4, 13312], P(None, ('enc', 'dp'))
- grad_w_img: float32 [2048, 768], replicated
- grad_w_box: float32 [4, 768], replicated
- grad_b_img: float32 [768], replicated
- grad_g_reg: float32 [768], replicated
- grad_beta_reg: float32 [768], replicated
- grad_w_query: float32 [768, 768], replicated
- grad_b_query: float32 [768], replicated
- grad_w_key: float32 [768, 768], replicated
- grad_w_value: float32 [768, 768], replicated
- grad_b_value: float32 [768], replicated
- grad_w_out: float32 [768, 768], replicated
- grad_b_out: float32 [768], replicated
- grad_g_one: float32 [768], replicated
- grad_beta_one: float32 [768], replicated
- grad_w_up: float32 [768, 3072], replicated
- grad_b_up: float32 [3072], replicated
- grad_w_down: float32 [3072, 768], replicated
- grad_b_down: float32 [768], replicated
- grad_g_two: float32 [768], replicated
- grad_beta_two: float32 [768], replicated
Inputs may be any that keep to these rules, and one draw needn't show every extreme that they name: `caption_count`: some sequence has exactly 128 caption tokens. `region_count`: in every draw some holder's 4 sequences all have 100 regions.
All inputs are finite; a program needn't handle non-finite values.
Results may differ from a plain program's by a relative error of at most 0.018.
Values may be sent and summed in bfloat16 or wider, within the bound.
No kernel may reach another device: no remote copies, remote signals or barrier semaphores. Data moves between devices by JAX's collectives and lax.ppermute only.
A program may use at most 192 MiB of HBM per device.

v0:
```python
import jax
import jax.numpy as jnp
from jax import lax
from jax.sharding import PartitionSpec as P

HEADS = 12
epsilon = 1e-05


def normalize(values, gain_vec, shift_vec):
    centered = values - jnp.mean(values, -1, keepdims=True)
    inverse = lax.rsqrt(jnp.mean(centered * centered, -1, keepdims=True) + epsilon)
    normed = centered * inverse
    return (normed * gain_vec + shift_vec, normed, inverse)


def normalize_back(upstream, normed, inverse, gain_vec):
    weighted = upstream * gain_vec
    result = inverse * (
        weighted
        - jnp.mean(weighted, -1, keepdims=True)
        - normed * jnp.mean(weighted * normed, -1, keepdims=True)
    )
    return (result, jnp.sum(upstream * normed, 0), jnp.sum(upstream, 0))


def exact_gelu(values):
    return jax.nn.gelu(values, approximate=False)


def outer_sum(row_data, row_grad):
    return jnp.einsum("ra,rb->ab", row_data, row_grad, preferred_element_type=jnp.float32)


def back_product(row_grad, weight):
    return jnp.einsum("rb,ab->ra", row_grad, weight, preferred_element_type=jnp.float32)


def column_sum(row_grad):
    return jnp.sum(row_grad.astype(jnp.float32), 0)


def body(
    text,
    region_feats,
    boxes,
    caption_count,
    region_count,
    region_offset,
    w_img,
    w_box,
    b_img,
    g_reg,
    beta_reg,
    w_query,
    b_query,
    w_key,
    w_value,
    b_value,
    w_out,
    b_out,
    g_one,
    beta_one,
    w_up,
    b_up,
    w_down,
    b_down,
    g_two,
    beta_two,
    cotangent,
):
    img_full, query_full, key_full, value_full, out_full, up_full, down_full = (
        lax.all_gather(w_img, ("enc", "dp"), axis=0, tiled=True),
        lax.all_gather(w_query, ("enc", "dp"), axis=0, tiled=True),
        lax.all_gather(w_key, ("enc", "dp"), axis=0, tiled=True),
        lax.all_gather(w_value, ("enc", "dp"), axis=0, tiled=True),
        lax.all_gather(w_out, ("enc", "dp"), axis=0, tiled=True),
        lax.all_gather(w_up, ("enc", "dp"), axis=0, tiled=True),
        lax.all_gather(w_down, ("enc", "dp"), axis=0, tiled=True),
    )
    device_count = lax.axis_size(("enc", "dp"))
    seq_count = caption_count.shape[0]
    model_width = text.shape[1]
    text_len = text.shape[0] // seq_count
    seq_len = cotangent.shape[0] // seq_count
    region_len = seq_len - text_len
    sent_rows = region_feats.shape[0]
    per_peer = sent_rows // device_count
    head_dim = model_width // HEADS
    score_scale = head_dim ** (-0.5)
    pre_norm = (
        jnp.dot(region_feats, img_full, preferred_element_type=jnp.float32)
        + jnp.einsum("cr,cd->rd", boxes, w_box, preferred_element_type=jnp.float32)
        + b_img
    )
    encoded, enc_normed, enc_inverse = normalize(pre_norm, g_reg, beta_reg)
    received = lax.all_to_all(
        encoded.astype(jnp.bfloat16), ("enc", "dp"), split_axis=0, concat_axis=0, tiled=True
    )
    position = jnp.arange(sent_rows, dtype=jnp.int32)
    arrival = (
        position % per_peer * device_count
        + (position // per_peer - region_offset[0]) % device_count
    )
    starts = jnp.cumsum(region_count) - region_count
    slot_total = seq_count * region_len
    slot_pos = jnp.arange(slot_total, dtype=jnp.int32) % region_len
    wanted = jnp.repeat(starts, region_len, total_repeat_length=slot_total) + slot_pos
    slot_live = slot_pos < jnp.repeat(region_count, region_len, total_repeat_length=slot_total)
    placement = ((wanted[:, None] == arrival[None, :]) & slot_live[:, None]).astype(jnp.bfloat16)
    regions = jnp.dot(placement, received, preferred_element_type=jnp.float32).astype(jnp.bfloat16)
    hidden_in = jnp.concatenate(
        [
            text.reshape(seq_count, text_len, model_width),
            regions.reshape(seq_count, region_len, model_width),
        ],
        1,
    ).reshape(seq_count * seq_len, model_width)
    key_live = jnp.concatenate(
        [
            jnp.arange(text_len)[None, :] < caption_count[:, None],
            jnp.arange(region_len)[None, :] < region_count[:, None],
        ],
        1,
    )
    row_live = key_live.reshape(-1, 1).astype(jnp.float32)

    def heads_view(tensor):
        return tensor.reshape(seq_count, seq_len, HEADS, head_dim)

    query_heads = heads_view(
        (jnp.dot(hidden_in, query_full, preferred_element_type=jnp.float32) + b_query).astype(
            jnp.bfloat16
        )
    )
    key_heads = heads_view(
        jnp.dot(hidden_in, key_full, preferred_element_type=jnp.float32).astype(jnp.bfloat16)
    )
    value_heads = heads_view(
        (jnp.dot(hidden_in, value_full, preferred_element_type=jnp.float32) + b_value).astype(
            jnp.bfloat16
        )
    )
    scores = (
        jnp.einsum("sqhd,skhd->shqk", query_heads, key_heads, preferred_element_type=jnp.float32)
        * score_scale
    )
    scores = jnp.where(key_live[:, None, None, :], scores, -1e30)
    row_max = jnp.max(scores, -1, keepdims=True)
    exp_scores = jnp.exp(scores - row_max)
    attn_probs = exp_scores / jnp.sum(exp_scores, -1, keepdims=True)
    probs_low = attn_probs.astype(jnp.bfloat16)
    context = (
        jnp.einsum("shqk,skhd->sqhd", probs_low, value_heads, preferred_element_type=jnp.float32)
        .reshape(-1, model_width)
        .astype(jnp.bfloat16)
    )
    mixed = (
        hidden_in.astype(jnp.float32)
        + jnp.dot(context, out_full, preferred_element_type=jnp.float32)
        + b_out
    )
    normed_one, one_normed, one_inverse = normalize(mixed, g_one, beta_one)
    normed_one = normed_one.astype(jnp.bfloat16)
    gate_in = jnp.dot(normed_one, up_full, preferred_element_type=jnp.float32) + b_up
    activated = exact_gelu(gate_in).astype(jnp.bfloat16)
    second_in = (
        normed_one.astype(jnp.float32)
        + jnp.dot(activated, down_full, preferred_element_type=jnp.float32)
        + b_down
    )
    normed_two, two_normed, two_inverse = normalize(second_in, g_two, beta_two)
    output = (normed_two * row_live).astype(jnp.bfloat16)
    grad_second = cotangent.astype(jnp.float32) * row_live
    grad_second_in, grad_g_two, grad_beta_two = normalize_back(
        grad_second, two_normed, two_inverse, g_two
    )
    grad_down_out = grad_second_in.astype(jnp.bfloat16)
    grad_w_down = outer_sum(activated, grad_down_out)
    grad_b_down = column_sum(grad_down_out)
    grad_activated = back_product(grad_down_out, down_full)
    gelu_pull = jax.vjp(exact_gelu, gate_in)[1]
    grad_gate = gelu_pull(grad_activated)[0].astype(jnp.bfloat16)
    grad_w_up = outer_sum(normed_one, grad_gate)
    grad_b_up = column_sum(grad_gate)
    grad_first = back_product(grad_gate, up_full) + grad_second_in
    grad_mixed, grad_g_one, grad_beta_one = normalize_back(
        grad_first, one_normed, one_inverse, g_one
    )
    grad_attn = grad_mixed.astype(jnp.bfloat16)
    grad_w_out = outer_sum(context, grad_attn)
    grad_b_out = column_sum(grad_attn)
    grad_context = heads_view(back_product(grad_attn, out_full).astype(jnp.bfloat16))
    grad_probs = jnp.einsum(
        "sqhd,skhd->shqk", grad_context, value_heads, preferred_element_type=jnp.float32
    )
    grad_values = (
        jnp.einsum("shqk,sqhd->skhd", probs_low, grad_context, preferred_element_type=jnp.float32)
        .reshape(-1, model_width)
        .astype(jnp.bfloat16)
    )
    grad_scores = (
        attn_probs * (grad_probs - jnp.sum(attn_probs * grad_probs, -1, keepdims=True))
    ).astype(jnp.bfloat16)
    grad_query = (
        (
            jnp.einsum(
                "shqk,skhd->sqhd", grad_scores, key_heads, preferred_element_type=jnp.float32
            )
            * score_scale
        )
        .reshape(-1, model_width)
        .astype(jnp.bfloat16)
    )
    grad_keys = (
        (
            jnp.einsum(
                "shqk,sqhd->skhd", grad_scores, query_heads, preferred_element_type=jnp.float32
            )
            * score_scale
        )
        .reshape(-1, model_width)
        .astype(jnp.bfloat16)
    )
    grad_w_query = outer_sum(hidden_in, grad_query)
    grad_b_query = column_sum(grad_query)
    grad_w_key = outer_sum(hidden_in, grad_keys)
    grad_w_value = outer_sum(hidden_in, grad_values)
    grad_b_value = column_sum(grad_values)
    grad_hidden = (
        grad_mixed
        + back_product(grad_query, query_full)
        + back_product(grad_keys, key_full)
        + back_product(grad_values, value_full)
    )
    grad_hidden = grad_hidden.reshape(seq_count, seq_len, model_width)
    grad_text = grad_hidden[:, :text_len].reshape(-1, model_width).astype(jnp.bfloat16)
    grad_slots = grad_hidden[:, text_len:].reshape(-1, model_width).astype(jnp.bfloat16)
    grad_sent = jnp.einsum(
        "tn,td->nd", placement, grad_slots, preferred_element_type=jnp.float32
    ).astype(jnp.bfloat16)
    grad_encoded = lax.all_to_all(
        grad_sent, ("enc", "dp"), split_axis=0, concat_axis=0, tiled=True
    ).astype(jnp.float32)
    grad_pre, grad_g_reg, grad_beta_reg = normalize_back(
        grad_encoded, enc_normed, enc_inverse, g_reg
    )
    grad_pre = grad_pre.astype(jnp.bfloat16)
    grad_w_img = outer_sum(region_feats, grad_pre)
    grad_w_box = jnp.einsum("cr,rd->cd", boxes, grad_pre, preferred_element_type=jnp.float32)
    grad_b_img = column_sum(grad_pre)
    grad_feats = back_product(grad_pre, img_full).astype(jnp.bfloat16)
    grad_boxes = jnp.einsum(
        "cd,rd->cr", w_box, grad_pre, preferred_element_type=jnp.float32
    ).astype(jnp.bfloat16)
    (
        grad_w_img,
        grad_w_box,
        grad_b_img,
        grad_g_reg,
        grad_beta_reg,
        grad_w_query,
        grad_b_query,
        grad_w_key,
        grad_w_value,
        grad_b_value,
        grad_w_out,
        grad_b_out,
        grad_g_one,
        grad_beta_one,
        grad_w_up,
        grad_b_up,
        grad_w_down,
        grad_b_down,
        grad_g_two,
        grad_beta_two,
    ) = lax.psum(
        (
            grad_w_img,
            grad_w_box,
            grad_b_img,
            grad_g_reg,
            grad_beta_reg,
            grad_w_query,
            grad_b_query,
            grad_w_key,
            grad_w_value,
            grad_b_value,
            grad_w_out,
            grad_b_out,
            grad_g_one,
            grad_beta_one,
            grad_w_up,
            grad_b_up,
            grad_w_down,
            grad_b_down,
            grad_g_two,
            grad_beta_two,
        ),
        ("enc", "dp"),
    )
    return (
        output,
        grad_text,
        grad_feats,
        grad_boxes,
        grad_w_img,
        grad_w_box,
        grad_b_img,
        grad_g_reg,
        grad_beta_reg,
        grad_w_query,
        grad_b_query,
        grad_w_key,
        grad_w_value,
        grad_b_value,
        grad_w_out,
        grad_b_out,
        grad_g_one,
        grad_beta_one,
        grad_w_up,
        grad_b_up,
        grad_w_down,
        grad_b_down,
        grad_g_two,
        grad_beta_two,
    )


def solution(mesh):
    return jax.shard_map(
        body,
        mesh=mesh,
        in_specs=(
            P(("enc", "dp"), None),
            P(("enc", "dp"), None),
            P(None, ("enc", "dp")),
            P(("enc", "dp")),
            P(("enc", "dp")),
            P(("enc", "dp")),
            P(("enc", "dp"), None),
            P(),
            P(),
            P(),
            P(),
            P(("enc", "dp"), None),
            P(),
            P(("enc", "dp"), None),
            P(("enc", "dp"), None),
            P(),
            P(("enc", "dp"), None),
            P(),
            P(),
            P(),
            P(("enc", "dp"), None),
            P(),
            P(("enc", "dp"), None),
            P(),
            P(),
            P(),
            P(("enc", "dp"), None),
        ),
        out_specs=(
            P(("enc", "dp"), None),
            P(("enc", "dp"), None),
            P(("enc", "dp"), None),
            P(None, ("enc", "dp")),
            P(),
            P(),
            P(),
            P(),
            P(),
            P(),
            P(),
            P(),
            P(),
            P(),
            P(),
            P(),
            P(),
            P(),
            P(),
            P(),
            P(),
            P(),
            P(),
            P(),
        ),
        check_vma=False,
    )
```

profile of v0, /device:TPU:0, one launch (start us, length us, event | category | flops | bytes accessed | tf_op | source)
XLA Modules:
  0.0 1141.4 jit_solution(5793821062588575223)
XLA Ops:
  11.2 61.4 %all-gather.8.cloned.1.call-done = bf16[2048,768]{1,0:T(8,128)(2,1)} async-done(((bf16[64,768]{1,0:T(8,128)(2,1)}), bf16[2048,768]{1,0:T(8,128)(2,1)}) %all-gather.8.cloned.1.call-update) | async-done | bytes 3145744 | tf_op jit(solution)/shard_map/all_gather | solution.py:73
  72.6 3.4 fusion.82
  79.5 3.4 all-to-all-start
  85.8 2.6 select_compare_fusion
  89.0 2.6 select_add_fusion
  91.7 12.7 %all-to-all-done = bf16[32,13,768]{2,1,0:T(8,128)(2,1)S(1)} async-done(((bf16[32,13,768]{2,1,0:T(8,128)(2,1)}), bf16[32,13,768]{2,1,0:T(8,128)(2,1)S(1)}, u32[]{:S(2)}, u32[]{:S(2)}) %all-to-all-start) | async-done | bytes 639008 | tf_op jit(solution)/shard_map/all_to_all | solution.py:97
  106.5 24.1 %all-gather.14.cloned.1.call-done = bf16[768,768]{1,0:T(8,128)(2,1)} async-done(((bf16[24,768]{1,0:T(8,128)(2,1)}), bf16[768,768]{1,0:T(8,128)(2,1)}) %all-gather.14.cloned.1.call-update) | async-done | bytes 1179664 | tf_op jit(solution)/shard_map/all_gather | solution.py:75
  130.7 3.8 convolution_convert_fusion.2
  134.5 1.7 copy.66
  136.2 2.4 reshape.314
  138.6 48.0 %all-gather.12.cloned.1.call-done = bf16[768,768]{1,0:T(8,128)(2,1)} async-done(((bf16[24,768]{1,0:T(8,128)(2,1)}), bf16[768,768]{1,0:T(8,128)(2,1)}) %all-gather.12.cloned.1.call-update) | async-done | bytes 1179664 | tf_op jit(solution)/shard_map/all_gather | solution.py:74
  186.6 3.1 add_convert_fusion.3
  189.7 1.6 copy.65
  191.4 2.9 reshape.313
  194.3 48.1 %all-gather.10.cloned.1.call-done = bf16[768,768]{1,0:T(8,128)(2,1)} async-done(((bf16[24,768]{1,0:T(8,128)(2,1)}), bf16[768,768]{1,0:T(8,128)(2,1)}) %all-gather.10.cloned.1.call-update) | async-done | bytes 1179664 | tf_op jit(solution)/shard_map/all_gather | solution.py:76
  242.3 4.3 add_convert_fusion.4
  246.6 2.6 copy.64
  249.2 3.9 reshape.312
  253.0 7.8 fusion.39
  260.8 12.9 %fusion.78 = (f32[4,12,256]{2,1,0:T(8,128)S(1)}, f32[4,12,256,256]{2,3,1,0:T(8,128)S(1)}) fusion(f32[4,12,256,256]{2,3,1,0:T(8,128)} %fusion.39, pred[4,256]{1,0:T(4,128)(4,1)S(1)} %get-tuple-element.137), kind=kOutput, calls=%fused_computation.163 | output fusion | flops 18874624 | bytes 25216000 | tf_op jit(solution)/shard_map/sub | solution.py:150
  274.9 3.4 copy-done.8
  279.7 1.5 copy.89
  281.2 16.9 %all-gather.16.cloned.1.call-done = bf16[768,768]{1,0:T(8,128)(2,1)} async-done(((bf16[24,768]{1,0:T(8,128)(2,1)}), bf16[768,768]{1,0:T(8,128)(2,1)}) %all-gather.16.cloned.1.call-update) | async-done | bytes 1179664 | tf_op jit(solution)/shard_map/all_gather | solution.py:77
  298.1 3.4 fusion.79
  301.6 1.6 copy-done.3
  303.8 59.7 %all-gather.18.cloned.1.call-done = bf16[768,3072]{1,0:T(8,128)(2,1)} async-done(((bf16[24,3072]{1,0:T(8,128)(2,1)}), bf16[768,3072]{1,0:T(8,128)(2,1)}) %all-gather.18.cloned.1.call-update) | async-done | bytes 4718608 | tf_op jit(solution)/shard_map/all_gather | solution.py:78
  363.4 38.1 %multiply_convert_fusion.1 = (bf16[1024,3072]{1,0:T(8,128)(2,1)}, f32[1024,3072]{1,0:T(8,128)}, f32[1024,3072]{1,0:T(8,128)}) fusion(f32[3072]{0:T(1024)S(1)} %copy-done.60, bf16[768,3072]{1,0:T(8,128)(2,1)} %all-gather.18.cloned.1.call-done, f32[1024,768]{1,0:T(8,128)} %copy-done.3, f32[768]{0:T(1024)S(1)} %copy-done.34, f32[768]{0:T(1024)S(1)} %copy-done.29, ...), kind=kOutput, calls=%fused_computation.7 | convolution fusion | flops 5043388416 | bytes 39348224 | tf_op jit(solution)/shard_map/dot_general | solution.py:165
  401.5 27.3 %all-gather.20.cloned.1.call-done = bf16[3072,768]{1,0:T(8,128)(2,1)} async-done(((bf16[96,768]{1,0:T(8,128)(2,1)}), bf16[3072,768]{1,0:T(8,128)(2,1)}) %all-gather.20.cloned.1.call-update) | async-done | bytes 4718608 | tf_op jit(solution)/shard_map/all_gather | solution.py:79
  428.8 9.3 fusion.80
  439.6 2.4 multiply_reduce_fusion.1
  442.0 3.7 convert_reduce_fusion.1
  445.8 7.8 fusion.68
  453.6 18.8 %convert_reduce_fusion = (f32[3072]{0:T(1024)S(1)}, bf16[1024,3072]{1,0:T(8,128)(2,1)}) fusion(f32[1024,3072]{1,0:T(8,128)} %get-tuple-element.132, bf16[3072,768]{1,0:T(8,128)(2,1)} %all-gather.20.cloned.1.call-done, f32[1024,768]{1,0:T(8,128)} %copy-done.15, f32[1024,3072]{1,0:T(8,128)} %get-tuple-element.152, f32[3072]{0:T(1024)S(1)} %copy-done.60), kind=kOutput, calls=%fused_computation.3 | convolution fusion | flops 4886098944 | bytes 39346176 | tf_op jit(solution)/shard_map/rb,ab->ra/dot_general | solution.py:36
  472.4 10.1 multiply_reduce_fusion.2
  483.9 2.8 fusion.65
  486.7 2.6 convolution_convert_fusion.1
  489.3 1.7 copy.72
  491.1 2.4 reshape.315
  493.4 7.3 convert_reduce_fusion.3
  500.8 8.9 multiply_reduce_fusion
  509.7 6.9 multiply_convert_fusion
  516.7 2.0 fusion.31
  521.6 2.9 fusion.87
  527.6 2.9 fusion.85
  530.5 2.9 fusion.86
  533.4 1.7 fusion.83
  535.1 1.5 fusion.84
  537.3 1.6 add_convert_fusion.1
  541.7 3.5 all-to-all-start.1
  545.3 11.0 fusion.81
  556.3 9.5 all-to-all-done.1
  565.9 1.5 convert_reduce_fusion.6
  567.5 2.3 reshape.319
  569.8 1.9 multiply_reduce_fusion.9
  573.0 4.5 convolution_bitcast_fusion
  578.8 43.5 %all-reduce = (f32[4,768]{1,0:T(4,128)}, f32[768]{0:T(1024)}, f32[768]{0:T(1024)}, f32[768]{0:T(1024)}, f32[768]{0:T(1024)}, /*index=5*/f32[768]{0:T(1024)}, f32...) all-reduce(f32[4,768]{1,0:T(4,128)S(1)} %convolution_bitcast_fusion, ...), channel_id=1, replica_groups=mesh['enc'=4,'dp'=8] {'enc','dp'}, use_global_device_ids=true, to_apply=%region_17.19 | all-reduce | flops 14592 | bytes 116736 | tf_op jit(solution)/shard_map/psum | solution.py:277
  623.3 4.9 convolution_convert_fusion
  628.2 476.7 %all-reduce.4.cloned.1.call-done = (f32[2048,768]{0,1:T(8,128)}, f32[768,768]{1,0:T(8,128)}, f32[768,768]{1,0:T(8,128)}, f32[768,768]{1,0:T(8,128)}, f32[768,768...) async-done(((f32[2048,768]{0,1:T(8,128)}, f32[768,768]{1,0:T(8,128)}, f32[768,768]{1,0:T(8,128)}, f32[768,768]{1,0:T(8,128)}, f32[768,768]{1,0:T(8,128)}, ...) | async-done | bytes 34603024 | tf_op jit(solution)/shard_map/psum | solution.py:277
  1104.9 6.6 copy.84
  1111.4 3.4 copy.126
  1114.8 1.4 copy.127
  1117.3 1.4 copy.128
  1121.2 9.3 copy.130
  1130.6 3.7 copy.131
  (212 shorter events, 35.1 us)
Async XLA Ops:
  7.2 65.4 %copy-start = (bf16[416,2048]{1,0:T(8,128)(2,1)S(1)}, bf16[416,2048]{1,0:T(8,128)(2,1)}, u32[]{:S(2)}) copy-start(bf16[416,2048]{1,0:T(8,128)(2,1)} %param.34) | copy-start | bytes 5111812
  7.2 65.4 %all-gather.8.cloned.1.call-start = ((), (), s32[]{:S(2)}) async-start(), calls=%async_computation.2 | async-start | bytes 3244032 | tf_op jit(solution)/shard_map/all_gather | solution.py:73
  7.9 122.7 %all-gather.14.cloned.1.call-start = ((), (), s32[]{:S(2)}) async-start(), calls=%async_computation.5 | async-start | bytes 1216512 | tf_op jit(solution)/shard_map/all_gather | solution.py:75
  8.7 177.9 %all-gather.12.cloned.1.call-start = ((), (), s32[]{:S(2)}) async-start(), calls=%async_computation.4 | async-start | bytes 1216512 | tf_op jit(solution)/shard_map/all_gather | solution.py:74
  9.4 232.9 %all-gather.10.cloned.1.call-start = ((), (), s32[]{:S(2)}) async-start(), calls=%async_computation.3 | async-start | bytes 1216512 | tf_op jit(solution)/shard_map/all_gather | solution.py:76
  10.0 288.1 %all-gather.16.cloned.1.call-start = ((), (), s32[]{:S(2)}) async-start(), calls=%async_computation.6 | async-start | bytes 1216512 | tf_op jit(solution)/shard_map/all_gather | solution.py:77
  10.6 352.9 %all-gather.18.cloned.1.call-start = ((), (), s32[]{:S(2)}) async-start(), calls=%async_computation.7 | async-start | bytes 4866048 | tf_op jit(solution)/shard_map/all_gather | solution.py:78
  11.2 64.8 %copy-start.38 = (bf16[4,768]{1,0:T(4,128)(2,1)S(1)}, bf16[4,768]{1,0:T(4,128)(2,1)}, u32[]{:S(2)}) copy-start(bf16[4,768]{1,0:T(4,128)(2,1)} %param.40) | copy-start | bytes 18436
  11.2 64.8 %copy-start.41 = (bf16[4,416]{1,0:T(4,128)(2,1)S(1)}, bf16[4,416]{1,0:T(4,128)(2,1)}, u32[]{:S(2)}) copy-start(bf16[4,416]{1,0:T(4,128)(2,1)} %param.35) | copy-start | bytes 9988
  11.2 64.8 %copy-start.47 = (f32[768]{0:T(1024)S(1)}, f32[768]{0:T(1024)}, u32[]{:S(2)}) copy-start(f32[768]{0:T(1024)} %param.41) | copy-start | bytes 9220
  76.0 2.1 copy-start.30
  76.0 2.1 copy-start.48
  76.5 7.8 copy-start.46
  76.5 7.8 copy-start.56
  79.5 24.9 %all-to-all-start = ((bf16[32,13,768]{2,1,0:T(8,128)(2,1)}), bf16[32,13,768]{2,1,0:T(8,128)(2,1)S(1)}, u32[]{:S(2)}, u32[]{:S(2)}) async-start(bf16[32,13,768]{2,1,0:T(8,128)(2,1)} %all_to_all.14), calls=%async_computation | async-start | bytes 1572864 | tf_op jit(solution)/shard_map/all_to_all | solution.py:97
  82.9 345.9 %all-gather.20.cloned.1.call-start = ((), (), s32[]{:S(2)}) async-start(), calls=%async_computation.8 | async-start | bytes 4866048 | tf_op jit(solution)/shard_map/all_gather | solution.py:79
  88.4 16.9 %copy-start.54 = (pred[512]{0:T(512)(128)(4,1)}, pred[512]{0:T(512)(128)(4,1)S(1)}, u32[]{:S(2)}) copy-start(pred[512]{0:T(512)(128)(4,1)S(1)} %select_compare_fusion) | copy-start | bytes 1540
  88.4 16.8 %copy-start.50 = (s32[416]{0:T(512)}, s32[416]{0:T(512)S(1)}, u32[]{:S(2)}) copy-start(s32[416]{0:T(512)S(1)} %fusion.52) | copy-start | bytes 4996
  91.6 13.6 %copy-start.52 = (s32[512]{0:T(512)}, s32[512]{0:T(512)S(1)}, u32[]{:S(2)}) copy-start(s32[512]{0:T(512)S(1)} %select_add_fusion) | copy-start | bytes 6148
  106.5 24.1 %copy-start.19 = (bf16[4,256,768]{2,1,0:T(8,128)(2,1)}, bf16[4,256,768]{2,1,0:T(8,128)(2,1)S(1)}, u32[]{:S(2)}) copy-start(bf16[4,256,768]{2,1,0:T(8,128)(2,1)S(1)} %pad_maximum_fusion) | copy-start | bytes 4718596
  134.5 52.1 %copy-start.61 = (f32[768]{0:T(1024)S(1)}, f32[768]{0:T(1024)}, u32[]{:S(2)}) copy-start(f32[768]{0:T(1024)} %param.45) | copy-start | bytes 9220
  189.7 52.6 %copy-start.62 = (f32[768]{0:T(1024)S(1)}, f32[768]{0:T(1024)}, u32[]{:S(2)}) copy-start(f32[768]{0:T(1024)} %param.48) | copy-start | bytes 9220
  194.2 58.8 %copy-start.5 = (bf16[4,256,12,64]{1,0,3,2:T(4,128)(2,1)}, bf16[4,256,12,64]{1,0,3,2:T(4,128)(2,1)S(1)}, u32[]{:S(2)}) copy-start(bf16[4,256,12,64]{1,0,3,2:T(4,128)(2,1)S(1)} %reshape.313) | copy-start | bytes 4718596
  260.8 12.9 %copy-start.22 = (bf16[4,256,12,64]{1,0,3,2:T(4,128)(2,1)S(1)}, bf16[4,256,12,64]{1,0,3,2:T(4,128)(2,1)}, u32[]{:S(2)}) copy-start(bf16[4,256,12,64]{1,0,3,2:T(4,128)(2,1)} %reshape.312) | copy-start | bytes 4718596
  273.7 4.5 copy-start.8
  273.7 4.8 copy-start.27
  278.5 19.6 %copy-start.20 = (bf16[4,256,768]{2,1,0:T(8,128)(2,1)S(1)}, bf16[4,256,768]{2,1,0:T(8,128)(2,1)}, u32[]{:S(2)}) copy-start(bf16[4,256,768]{2,1,0:T(8,128)(2,1)} %copy-done.19) | copy-start | bytes 4718596
  278.5 19.6 %copy-start.63 = (f32[768]{0:T(1024)S(1)}, f32[768]{0:T(1024)}, u32[]{:S(2)}) copy-start(f32[768]{0:T(1024)} %param.50) | copy-start | bytes 9220
  301.5 61.9 %copy-start.29 = (f32[768]{0:T(1024)S(1)}, f32[768]{0:T(1024)}, u32[]{:S(2)}) copy-start(f32[768]{0:T(1024)} %param.51) | copy-start | bytes 9220
  301.5 61.9 %copy-start.34 = (f32[768]{0:T(1024)S(1)}, f32[768]{0:T(1024)}, u32[]{:S(2)}) copy-start(f32[768]{0:T(1024)} %param.52) | copy-start | bytes 9220
  301.5 61.9 %copy-start.60 = (f32[3072]{0:T(1024)S(1)}, f32[3072]{0:T(1024)}, u32[]{:S(2)}) copy-start(f32[3072]{0:T(1024)} %param.54) | copy-start | bytes 36868
  303.7 125.1 %copy-start.64 = (f32[768]{0:T(1024)S(1)}, f32[768]{0:T(1024)}, u32[]{:S(2)}) copy-start(f32[768]{0:T(1024)} %param.56) | copy-start | bytes 9220
  438.7 3.3 copy-start.49
  439.6 6.2 slice-start.6
  442.0 3.7 slice-start.7
  445.8 7.8 copy-start.15
  453.6 18.8 %copy-start.4 = (f32[1024,768]{1,0:T(8,128)S(1)}, f32[1024,768]{1,0:T(8,128)}, u32[]{:S(2)}) copy-start(f32[1024,768]{1,0:T(8,128)} %copy-done.3) | copy-start | bytes 9437188
  483.6 3.1 copy-start.9
  483.9 2.8 copy-start.59
  489.3 4.1 copy-start.28
  493.4 7.3 copy-start.23
  493.4 7.4 copy-start.25
  493.4 16.3 %slice-start = ((s8[12582912]{0:T(1024)(128)(4,1)}), s8[4194304]{0:T(1024)(128)(4,1)S(1)}, s32[]{:S(2)}) async-start(s8[12582912]{0:T(1024)(128)(4,1)} %bitcast.136), calls=%async_computation.10 | async-start | bytes 8388608
  493.4 16.3 %slice-start.1 = ((s8[12582912]{0:T(1024)(128)(4,1)}), s8[4194304]{0:T(1024)(128)(4,1)S(1)}, s32[]{:S(2)}) async-start(s8[12582912]{0:T(1024)(128)(4,1)} %bitcast.136), calls=%async_computation.11 | async-start | bytes 8388608
  500.8 8.9 slice-start.2
  509.7 6.9 copy-start.6
  516.7 2.0 copy-start.7
  530.5 2.9 copy-start.58
  535.1 1.9 copy-start.10
  535.1 2.2 copy-start.26
  541.7 24.1 %all-to-all-start.1 = ((bf16[32,13,768]{2,1,0:T(8,128)(2,1)}), bf16[32,13,768]{2,1,0:T(8,128)(2,1)}, u32[]{:S(2)}, u32[]{:S(2)}) async-start(bf16[32,13,768]{2,1,0:T(8,128)(2,1)} %all_to_all.17), calls=%async_computation.1 | async-start | bytes 1572864 | tf_op jit(solution)/shard_map/all_to_all | solution.py:242
  545.2 20.6 %copy-start.31 = (f32[768]{0:T(1024)S(1)}, f32[768]{0:T(1024)}, u32[]{:S(2)}) copy-start(f32[768]{0:T(1024)} %param.42) | copy-start | bytes 9220
  545.3 24.5 %copy-start.33 = (f32[416]{0:T(512)S(1)}, f32[416]{0:T(512)}, u32[]{:S(2)}) copy-start(f32[416]{0:T(512)} %copy-done.32) | copy-start | bytes 4996
  545.3 24.5 %copy-start.37 = (f32[416]{0:T(512)S(1)}, f32[416]{0:T(512)}, u32[]{:S(2)}) copy-start(f32[416]{0:T(512)} %copy-done.36) | copy-start | bytes 4996
  545.3 559.6 %all-reduce.4.cloned.1.call-start = ((), (), s32[]{:S(2)}) async-start(), calls=%async_computation.9 | async-start | bytes 69206016 | tf_op jit(solution)/shard_map/psum | solution.py:277
  556.3 13.5 %copy-start.2 = (f32[416,768]{1,0:T(8,128)S(1)}, f32[416,768]{1,0:T(8,128)}, u32[]{:S(2)}) copy-start(f32[416,768]{1,0:T(8,128)} %copy-done.1) | copy-start | bytes 3833860
  569.8 1.9 copy-start.11
  577.6 44.8 %copy-start.39 = (bf16[4,768]{1,0:T(4,128)(2,1)S(1)}, bf16[4,768]{1,0:T(4,128)(2,1)}, u32[]{:S(2)}) copy-start(bf16[4,768]{1,0:T(4,128)(2,1)} %param.40) | copy-start | bytes 18436
  1111.4 3.4 copy-start.18
  1114.8 2.5 copy-start.17
  1117.3 2.5 copy-start.16
  1119.8 10.7 slice-start.3
  1121.2 9.3 slice-start.4
  1121.2 9.3 slice-start.5
  (19 other events, 23.1 us)
Sparse Core Ops, SparseCore 0:
  10.9 61.6 all-gather.7
  75.5 55.1 all-gather.13
  133.6 52.9 all-gather.11
  189.3 52.9 all-gather.9
  245.1 52.9 all-gather.15
  300.8 62.5 all-gather.17
  366.3 62.4 all-gather.19
  577.7 527.0 all-reduce.3
where the time goes:
time: 1150 us; the launch traced here: 1140 us
  waiting for transfers between devices  788 us (69%)
  matrix products  173 us (15%)
  local copies, waits for them, and re-layouts  74.1 us (6%)
  blocking collectives  43.5 us (4%)
  other arithmetic  39.3 us (3%)
  between operations  16 us (1%)
    psum x1, waiting for transfers between devices, body(): lax.psum((grad_w_img, grad_w_box, grad_b_img, grad_g_reg, grad_beta_reg,...  477 us
    all_gather x1, waiting for transfers between devices, body(): lax.all_gather(w_img, ('enc', 'dp'), axis=0, tiled=True)  61.4 us
    all_gather x1, waiting for transfers between devices, body(): lax.all_gather(w_up, ('enc', 'dp'), axis=0, tiled=True)  59.7 us
    all_gather x1, waiting for transfers between devices, body(): lax.all_gather(w_value, ('enc', 'dp'), axis=0, tiled=True)  48.1 us
    all_gather x1, waiting for transfers between devices, body(): lax.all_gather(w_query, ('enc', 'dp'), axis=0, tiled=True)  48 us
    psum x1, blocking collectives, body(): lax.psum((grad_w_img, grad_w_box, grad_b_img, grad_g_reg, grad_beta_reg,...  43.5 us
    unnamed x158, local copies, waits for them, and re-layouts  43 us
    dot_general x7, matrix products, back_product(): jnp.einsum('rb,ab->ra', row_grad, weight, preferred_element_type=jnp.floa...  41 us
  transfers between devices with their start and end apart: 10, of which 10 were waited for; matrix products, arithmetic and copies ran while one was open for 11% of the time, Pallas kernels for 0%

commit v1 on v0

--- a/solution.py
+++ b/solution.py
@@ -5,6 +5,18 @@
 
 HEADS = 12
 epsilon = 1e-05
+
+
+def collect(x, axis, dim):
+    ways, here = (lax.axis_size(axis), lax.axis_index(axis))
+    grown, reach = (x, 1)
+    while reach < ways:
+        theirs = lax.ppermute(grown, axis, [(d, d ^ reach) for d in range(ways)])
+        mine_first = jnp.concatenate([grown, theirs], axis=dim)
+        theirs_first = jnp.concatenate([theirs, grown], axis=dim)
+        grown = jnp.where(here & reach == 0, mine_first, theirs_first)
+        reach = 2 * reach
+    return grown
 
 
 def normalize(values, gain_vec, shift_vec):
@@ -76,7 +88,7 @@
         lax.all_gather(w_value, ("enc", "dp"), axis=0, tiled=True),
         lax.all_gather(w_out, ("enc", "dp"), axis=0, tiled=True),
         lax.all_gather(w_up, ("enc", "dp"), axis=0, tiled=True),
-        lax.all_gather(w_down, ("enc", "dp"), axis=0, tiled=True),
+        collect(w_down, ("enc", "dp"), 0),
     )
     device_count = lax.axis_size(("enc", "dp"))
     seq_count = caption_count.shape[0]

time: 1150 us -> 1220 us (1.061)
  waiting for transfers between devices: 788 us -> 843 us
    all_to_all x1, waiting for transfers between devices: 12.7 us -> 59.9 us  [body(): lax.all_to_all(encoded.astype(jnp.bfloat16), ('enc', 'dp'), split_axis=0,...]
    all_gather x1, waiting for transfers between devices: 24.1 us -> 65.5 us  [body(): lax.all_gather(w_key, ('enc', 'dp'), axis=0, tiled=True)]
    all_gather x1 -> x0, waiting for transfers between devices: 27.3 us -> none  [body(): lax.all_gather(w_down, ('enc', 'dp'), axis=0, tiled=True)]
    all_gather x1, waiting for transfers between devices: 61.4 us -> 34.1 us  [body(): lax.all_gather(w_img, ('enc', 'dp'), axis=0, tiled=True)]
    ppermute x0 -> x5, waiting for transfers between devices: none -> 21.7 us  [collect(): theirs = lax.ppermute(grown, axis, [(d, d ^ reach) for d in range(ways)])]
    unnamed x158 -> x154, local copies, waits for them, and re-layouts: 43 us -> 42.9 us
  transfers between devices with their start and end apart: 10 -> 14, of which waited for: 10 -> 12; matrix products, arithmetic and copies ran while one was open for 11% -> 11% of each run, Pallas kernels for 0% -> 0%
where the time goes in v1:
time: 1220 us
  waiting for transfers between devices  843 us (69%)
  matrix products  174 us (14%)
  local copies, waits for them, and re-layouts  75.2 us (6%)
  other arithmetic  44.1 us (4%)
  blocking collectives  43.5 us (4%)
  starting transfers between devices  19.8 us (2%)
  between operations  15.9 us (1%)
    psum x1, waiting for transfers between devices, body(): lax.psum((grad_w_img, grad_w_box, grad_b_img, grad_g_reg, grad_beta_reg,...  477 us
    all_gather x1, waiting for transfers between devices, body(): lax.all_gather(w_key, ('enc', 'dp'), axis=0, tiled=True)  65.5 us
    all_to_all x1, waiting for transfers between devices, body(): lax.all_to_all(encoded.astype(jnp.bfloat16), ('enc', 'dp'), split_axis=0,...  59.9 us
    all_gather x1, waiting for transfers between devices, body(): lax.all_gather(w_up, ('enc', 'dp'), axis=0, tiled=True)  59.7 us
    all_gather x1, waiting for transfers between devices, body(): lax.all_gather(w_value, ('enc', 'dp'), axis=0, tiled=True)  48.1 us
    all_gather x1, waiting for transfers between devices, body(): lax.all_gather(w_query, ('enc', 'dp'), axis=0, tiled=True)  48 us
    psum x1, blocking collectives, body(): lax.psum((grad_w_img, grad_w_box, grad_b_img, grad_g_reg, grad_beta_reg,...  43.5 us
    unnamed x154, local copies, waits for them, and re-layouts  42.9 us
  transfers between devices with their start and end apart: 14, of which 12 were waited for; matrix products, arithmetic and copies ran while one was open for 11% of the time, Pallas kernels for 0%

profile of v1, /device:TPU:0, one launch (start us, length us, event | category | flops | bytes accessed | tf_op | source)
XLA Modules:
  0.0 1215.7 jit_solution(16083378988239240381)
XLA Ops:
  13.4 2.9 collective-permute-start.1
  16.3 7.3 collective-permute-done.1
  23.8 1.8 collective-permute-start.2
  25.7 13.2 %collective-permute-done.2 = bf16[384,768]{1,0:T(8,128)(2,1)} collective-permute-done((bf16[384,768]{1,0:T(8,128)(2,1)S(1)}, bf16[384,768]{1,0:T(8,128)(2,1)}, u32[]{:S(2)}, u32[]{:S(2)}) %collective-permute-start.2) | collective-permute-done | bytes 589856 | tf_op jit(solution)/shard_map/ppermute | solution.py:14
  38.9 1.6 maximum_select_fusion.2
  42.1 34.1 %all-gather.7.cloned.1.call-done = bf16[2048,768]{1,0:T(8,128)(2,1)} async-done(((bf16[64,768]{1,0:T(8,128)(2,1)}), bf16[2048,768]{1,0:T(8,128)(2,1)}) %all-gather.7.cloned.1.call-update) | async-done | bytes 3145744 | tf_op jit(solution)/shard_map/all_gather | solution.py:85
  76.2 3.4 fusion.84
  83.1 6.4 all-to-all-start
  91.7 2.6 select_compare_fusion
  94.9 2.6 select_add_fusion
  97.5 2.9 maximum_select_fusion.1
  100.5 2.8 collective-permute-start.4
  103.3 59.9 %all-to-all-done = bf16[32,13,768]{2,1,0:T(8,128)(2,1)} async-done(((bf16[32,13,768]{2,1,0:T(8,128)(2,1)}), bf16[32,13,768]{2,1,0:T(8,128)(2,1)}, u32[]{:S(2)}, u32[]{:S(2)}) %all-to-all-start) | async-done | bytes 639008 | tf_op jit(solution)/shard_map/all_to_all | solution.py:109
  166.5 65.5 %all-gather.13.cloned.1.call-done = bf16[768,768]{1,0:T(8,128)(2,1)} async-done(((bf16[24,768]{1,0:T(8,128)(2,1)}), bf16[768,768]{1,0:T(8,128)(2,1)}) %all-gather.13.cloned.1.call-update) | async-done | bytes 1179664 | tf_op jit(solution)/shard_map/all_gather | solution.py:87
  232.1 3.8 convolution_convert_fusion.2
  235.9 1.7 copy.66
  237.6 2.4 reshape.314
  240.0 48.0 %all-gather.11.cloned.1.call-done = bf16[768,768]{1,0:T(8,128)(2,1)} async-done(((bf16[24,768]{1,0:T(8,128)(2,1)}), bf16[768,768]{1,0:T(8,128)(2,1)}) %all-gather.11.cloned.1.call-update) | async-done | bytes 1179664 | tf_op jit(solution)/shard_map/all_gather | solution.py:86
  288.0 3.1 add_convert_fusion.3
  291.1 1.6 copy.65
  292.7 2.9 reshape.313
  295.6 48.1 %all-gather.9.cloned.1.call-done = bf16[768,768]{1,0:T(8,128)(2,1)} async-done(((bf16[24,768]{1,0:T(8,128)(2,1)}), bf16[768,768]{1,0:T(8,128)(2,1)}) %all-gather.9.cloned.1.call-update) | async-done | bytes 1179664 | tf_op jit(solution)/shard_map/all_gather | solution.py:88
  343.7 4.3 add_convert_fusion.4
  348.0 2.6 copy.64
  350.6 3.9 reshape.312
  354.4 7.8 fusion.39
  362.2 12.9 %fusion.80 = (f32[4,12,256]{2,1,0:T(8,128)S(1)}, f32[4,12,256,256]{2,3,1,0:T(8,128)S(1)}) fusion(f32[4,12,256,256]{2,3,1,0:T(8,128)} %fusion.39, pred[4,256]{1,0:T(4,128)(4,1)S(1)} %get-tuple-element.137), kind=kOutput, calls=%fused_computation.170 | output fusion | flops 18874624 | bytes 25216000 | tf_op jit(solution)/shard_map/sub | solution.py:162
  376.2 3.4 copy-done.8
  382.6 16.9 %all-gather.15.cloned.1.call-done = bf16[768,768]{1,0:T(8,128)(2,1)} async-done(((bf16[24,768]{1,0:T(8,128)(2,1)}), bf16[768,768]{1,0:T(8,128)(2,1)}) %all-gather.15.cloned.1.call-update) | async-done | bytes 1179664 | tf_op jit(solution)/shard_map/all_gather | solution.py:89
  399.5 3.4 fusion.81
  403.0 1.6 copy-done.3
  405.1 59.7 %all-gather.17.cloned.1.call-done = bf16[768,3072]{1,0:T(8,128)(2,1)} async-done(((bf16[24,3072]{1,0:T(8,128)(2,1)}), bf16[768,3072]{1,0:T(8,128)(2,1)}) %all-gather.17.cloned.1.call-update) | async-done | bytes 4718608 | tf_op jit(solution)/shard_map/all_gather | solution.py:90
  464.8 37.6 %multiply_convert_fusion.1 = (bf16[1024,3072]{1,0:T(8,128)(2,1)S(1)}, f32[1024,3072]{1,0:T(8,128)}, f32[1024,3072]{1,0:T(8,128)}) fusion(f32[3072]{0:T(1024)S(1)} %copy-done.60, bf16[768,3072]{1,0:T(8,128)(2,1)} %all-gather.17.cloned.1.call-done, f32[1024,768]{1,0:T(8,128)} %copy-done.3, f32[768]{0:T(1024)S(1)} %copy-done.35, f32[768]{0:T(1024)S(1)} %copy-done.30, ...), kind=kOutput, calls=%fused_computation.7 | convolution fusion | flops 5043388416 | bytes 39348224 | tf_op jit(solution)/shard_map/dot_general | solution.py:177
  502.5 10.8 fusion.82
  514.8 2.4 multiply_reduce_fusion.1
  517.2 2.7 convert_reduce_fusion.1
  519.9 7.8 fusion.70
  527.7 17.3 %convert_reduce_fusion = (f32[3072]{0:T(1024)S(1)}, bf16[1024,3072]{1,0:T(8,128)(2,1)S(1)}) fusion(f32[1024,3072]{1,0:T(8,128)} %get-tuple-element.132, bf16[1536,768]{1,0:T(8,128)(2,1)} %collective-permute-done.4, bf16[1536,768]{1,0:T(8,128)(2,1)} %maximum_select_fusion.1, pred[]{:T(512)S(6)} %eq.36, f32[1024,768]{1,0:T(8,128)} %copy-done.16, ...), kind=kOutput, calls=%fused_computation.3 | convolution fusion | flops 4907332608 | bytes 39346176 | tf_op jit(solution)/shard_map/rb,ab->ra/dot_general | solution.py:48
  545.0 11.6 multiply_reduce_fusion.2
  558.1 2.8 fusion.67
  560.9 2.6 convolution_convert_fusion.1
  563.5 1.7 copy.72
  565.2 2.4 reshape.315
  567.6 7.3 convert_reduce_fusion.3
  575.0 8.9 multiply_reduce_fusion
  583.9 6.9 multiply_convert_fusion
  590.9 2.0 fusion.31
  595.8 2.9 fusion.89
  601.9 2.9 fusion.87
  604.7 2.9 fusion.88
  607.6 1.9 fusion.85
  616.1 3.5 all-to-all-start.1
  619.7 11.0 fusion.83
  630.7 9.5 all-to-all-done.1
  641.9 2.3 reshape.319
  644.2 1.9 multiply_reduce_fusion.9
  647.4 4.5 convolution_bitcast_fusion
  653.2 43.5 %all-reduce = (f32[4,768]{1,0:T(4,128)}, f32[768]{0:T(1024)}, f32[768]{0:T(1024)}, f32[768]{0:T(1024)}, f32[768]{0:T(1024)}, /*index=5*/f32[768]{0:T(1024)}, f32...) all-reduce(f32[4,768]{1,0:T(4,128)S(1)} %convolution_bitcast_fusion, ...), channel_id=1, replica_groups=mesh['enc'=4,'dp'=8] {'enc','dp'}, use_global_device_ids=true, to_apply=%region_17.19 | all-reduce | flops 14592 | bytes 116736 | tf_op jit(solution)/shard_map/psum | solution.py:289
  697.6 4.9 convolution_convert_fusion
  702.5 476.8 %all-reduce.4.cloned.1.call-done = (f32[2048,768]{0,1:T(8,128)}, f32[768,768]{1,0:T(8,128)}, f32[768,768]{1,0:T(8,128)}, f32[768,768]{1,0:T(8,128)}, f32[768,768...) async-done(((f32[2048,768]{0,1:T(8,128)}, f32[768,768]{1,0:T(8,128)}, f32[768,768]{1,0:T(8,128)}, f32[768,768]{1,0:T(8,128)}, f32[768,768]{1,0:T(8,128)}, ...) | async-done | bytes 34603024 | tf_op jit(solution)/shard_map/psum | solution.py:289
  1179.3 6.6 copy.84
  1185.8 3.4 copy.126
  1195.6 9.3 copy.130
  1205.0 3.7 copy.131
  (218 shorter events, 48.4 us)
Async XLA Ops:
  7.2 69.0 %copy-start = (bf16[416,2048]{1,0:T(8,128)(2,1)S(1)}, bf16[416,2048]{1,0:T(8,128)(2,1)}, u32[]{:S(2)}) copy-start(bf16[416,2048]{1,0:T(8,128)(2,1)} %param.34) | copy-start | bytes 5111812
  7.2 69.0 %all-gather.7.cloned.1.call-start = ((), (), s32[]{:S(2)}) async-start(), calls=%async_computation.2 | async-start | bytes 3244032 | tf_op jit(solution)/shard_map/all_gather | solution.py:85
  7.9 224.1 %all-gather.13.cloned.1.call-start = ((), (), s32[]{:S(2)}) async-start(), calls=%async_computation.5 | async-start | bytes 1216512 | tf_op jit(solution)/shard_map/all_gather | solution.py:87
  8.7 279.3 %all-gather.11.cloned.1.call-start = ((), (), s32[]{:S(2)}) async-start(), calls=%async_computation.4 | async-start | bytes 1216512 | tf_op jit(solution)/shard_map/all_gather | solution.py:86
  9.4 334.3 %all-gather.9.cloned.1.call-start = ((), (), s32[]{:S(2)}) async-start(), calls=%async_computation.3 | async-start | bytes 1216512 | tf_op jit(solution)/shard_map/all_gather | solution.py:88
  10.0 389.5 %all-gather.15.cloned.1.call-start = ((), (), s32[]{:S(2)}) async-start(), calls=%async_computation.6 | async-start | bytes 1216512 | tf_op jit(solution)/shard_map/all_gather | solution.py:89
  10.6 454.2 %all-gather.17.cloned.1.call-start = ((), (), s32[]{:S(2)}) async-start(), calls=%async_computation.7 | async-start | bytes 4866048 | tf_op jit(solution)/shard_map/all_gather | solution.py:90
  10.6 1.7 collective-permute-start
  13.4 10.2 collective-permute-start.1
  23.8 15.0 %collective-permute-start.2 = (bf16[384,768]{1,0:T(8,128)(2,1)S(1)}, bf16[384,768]{1,0:T(8,128)(2,1)}, u32[]{:S(2)}, u32[]{:S(2)}) collective-permute-start(bf16[384,768]{1,0:T(8,128)(2,1)S(1)} %maximum_select_fusion.5), channel_id=1, source_target_pairs={{0,4},{1,5},{2,6},{3,7},{4,0},{5,1},{6,2},{7,3},{8,12},{9,13},{10,... | collective-permute-start | bytes 1769480 | tf_op jit(solution)/shard_map/ppermute | solution.py:14
  40.5 39.1 %copy-start.39 = (bf16[4,768]{1,0:T(4,128)(2,1)S(1)}, bf16[4,768]{1,0:T(4,128)(2,1)}, u32[]{:S(2)}) copy-start(bf16[4,768]{1,0:T(4,128)(2,1)} %param.40) | copy-start | bytes 18436
  40.5 39.1 %copy-start.42 = (bf16[4,416]{1,0:T(4,128)(2,1)S(1)}, bf16[4,416]{1,0:T(4,128)(2,1)}, u32[]{:S(2)}) copy-start(bf16[4,416]{1,0:T(4,128)(2,1)} %param.35) | copy-start | bytes 9988
  40.5 39.1 %copy-start.47 = (f32[768]{0:T(1024)S(1)}, f32[768]{0:T(1024)}, u32[]{:S(2)}) copy-start(f32[768]{0:T(1024)} %param.41) | copy-start | bytes 9220
  40.5 57.0 %collective-permute-start.3 = (bf16[768,768]{1,0:T(8,128)(2,1)S(1)}, bf16[768,768]{1,0:T(8,128)(2,1)}, u32[]{:S(2)}, u32[]{:S(2)}) collective-permute-start(bf16[768,768]{1,0:T(8,128)(2,1)S(1)} %maximum_select_fusion.2), channel_id=1, source_target_pairs={{0,8},{1,9},{2,10},{3,11},{4,12},{5,13},{6,14},{7,15},{8,0},{9,1},... | collective-permute-start | bytes 3538952 | tf_op jit(solution)/shard_map/ppermute | solution.py:14
  79.6 2.2 copy-start.31
  79.6 2.1 copy-start.48
  80.1 9.4 copy-start.46
  80.2 9.4 copy-start.56
  83.1 80.1 %all-to-all-start = ((bf16[32,13,768]{2,1,0:T(8,128)(2,1)}), bf16[32,13,768]{2,1,0:T(8,128)(2,1)}, u32[]{:S(2)}, u32[]{:S(2)}) async-start(bf16[32,13,768]{2,1,0:T(8,128)(2,1)} %all_to_all.14), calls=%async_computation | async-start | bytes 1572864 | tf_op jit(solution)/shard_map/all_to_all | solution.py:109
  94.3 71.0 %copy-start.54 = (pred[512]{0:T(512)(128)(4,1)}, pred[512]{0:T(512)(128)(4,1)S(1)}, u32[]{:S(2)}) copy-start(pred[512]{0:T(512)(128)(4,1)S(1)} %select_compare_fusion) | copy-start | bytes 1540
  94.3 70.9 %copy-start.50 = (s32[416]{0:T(512)}, s32[416]{0:T(512)S(1)}, u32[]{:S(2)}) copy-start(s32[416]{0:T(512)S(1)} %fusion.52) | copy-start | bytes 4996
  97.5 67.7 %copy-start.52 = (s32[512]{0:T(512)}, s32[512]{0:T(512)S(1)}, u32[]{:S(2)}) copy-start(s32[512]{0:T(512)S(1)} %select_add_fusion) | copy-start | bytes 6148
  100.5 402.0 %collective-permute-start.4 = (bf16[1536,768]{1,0:T(8,128)(2,1)}, bf16[1536,768]{1,0:T(8,128)(2,1)}, u32[]{:S(2)}, u32[]{:S(2)}) collective-permute-start(bf16[1536,768]{1,0:T(8,128)(2,1)} %maximum_select_fusion.1), channel_id=1, source_target_pairs={{0,16},{1,17},{2,18},{3,19},{4,20},{5,21},{6,22},{7,23},{8,24},{9,... | collective-permute-start | bytes 7077896 | tf_op jit(solution)/shard_map/ppermute | solution.py:14
  166.5 65.6 %copy-start.20 = (bf16[4,256,768]{2,1,0:T(8,128)(2,1)}, bf16[4,256,768]{2,1,0:T(8,128)(2,1)S(1)}, u32[]{:S(2)}) copy-start(bf16[4,256,768]{2,1,0:T(8,128)(2,1)S(1)} %pad_maximum_fusion) | copy-start | bytes 4718596
  235.9 52.1 %copy-start.61 = (f32[768]{0:T(1024)S(1)}, f32[768]{0:T(1024)}, u32[]{:S(2)}) copy-start(f32[768]{0:T(1024)} %param.45) | copy-start | bytes 9220
  291.1 52.6 %copy-start.62 = (f32[768]{0:T(1024)S(1)}, f32[768]{0:T(1024)}, u32[]{:S(2)}) copy-start(f32[768]{0:T(1024)} %param.48) | copy-start | bytes 9220
  295.6 58.8 %copy-start.5 = (bf16[4,256,12,64]{1,0,3,2:T(4,128)(2,1)}, bf16[4,256,12,64]{1,0,3,2:T(4,128)(2,1)S(1)}, u32[]{:S(2)}) copy-start(bf16[4,256,12,64]{1,0,3,2:T(4,128)(2,1)S(1)} %reshape.313) | copy-start | bytes 4718596
  362.2 12.9 %copy-start.23 = (bf16[4,256,12,64]{1,0,3,2:T(4,128)(2,1)S(1)}, bf16[4,256,12,64]{1,0,3,2:T(4,128)(2,1)}, u32[]{:S(2)}) copy-start(bf16[4,256,12,64]{1,0,3,2:T(4,128)(2,1)} %reshape.312) | copy-start | bytes 4718596
  375.1 4.5 copy-start.8
  375.1 4.8 copy-start.28
  379.9 19.6 %copy-start.21 = (bf16[4,256,768]{2,1,0:T(8,128)(2,1)S(1)}, bf16[4,256,768]{2,1,0:T(8,128)(2,1)}, u32[]{:S(2)}) copy-start(bf16[4,256,768]{2,1,0:T(8,128)(2,1)} %copy-done.20) | copy-start | bytes 4718596
  379.9 19.6 %copy-start.63 = (f32[768]{0:T(1024)S(1)}, f32[768]{0:T(1024)}, u32[]{:S(2)}) copy-start(f32[768]{0:T(1024)} %param.50) | copy-start | bytes 9220
  402.9 61.9 %copy-start.30 = (f32[768]{0:T(1024)S(1)}, f32[768]{0:T(1024)}, u32[]{:S(2)}) copy-start(f32[768]{0:T(1024)} %param.51) | copy-start | bytes 9220
  402.9 61.9 %copy-start.35 = (f32[768]{0:T(1024)S(1)}, f32[768]{0:T(1024)}, u32[]{:S(2)}) copy-start(f32[768]{0:T(1024)} %param.52) | copy-start | bytes 9220
  402.9 61.9 %copy-start.60 = (f32[3072]{0:T(1024)S(1)}, f32[3072]{0:T(1024)}, u32[]{:S(2)}) copy-start(f32[3072]{0:T(1024)} %param.54) | copy-start | bytes 36868
  405.1 97.4 %copy-start.64 = (f32[768]{0:T(1024)S(1)}, f32[768]{0:T(1024)}, u32[]{:S(2)}) copy-start(f32[768]{0:T(1024)} %param.56) | copy-start | bytes 9220
  464.8 37.7 %copy-start.4 = (f32[1024,768]{1,0:T(8,128)S(1)}, f32[1024,768]{1,0:T(8,128)}, u32[]{:S(2)}) copy-start(f32[1024,768]{1,0:T(8,128)} %copy-done.3) | copy-start | bytes 9437188
  513.9 3.3 copy-start.49
  519.9 7.8 copy-start.16
  545.0 11.6 copy-start.12
  557.8 3.1 copy-start.9
  558.1 2.8 copy-start.59
  563.5 4.1 copy-start.29
  567.6 7.3 copy-start.24
  567.6 7.4 copy-start.26
  567.6 16.3 %slice-start = ((s8[12582912]{0:T(1024)(128)(4,1)}), s8[4194304]{0:T(1024)(128)(4,1)S(1)}, s32[]{:S(2)}) async-start(s8[12582912]{0:T(1024)(128)(4,1)} %bitcast.134), calls=%async_computation.9 | async-start | bytes 8388608
  567.6 16.3 %slice-start.1 = ((s8[12582912]{0:T(1024)(128)(4,1)}), s8[4194304]{0:T(1024)(128)(4,1)S(1)}, s32[]{:S(2)}) async-start(s8[12582912]{0:T(1024)(128)(4,1)} %bitcast.134), calls=%async_computation.10 | async-start | bytes 8388608
  575.0 8.9 slice-start.2
  583.9 7.0 copy-start.6
  604.7 2.9 copy-start.58
  609.5 2.2 copy-start.27
  616.1 24.1 %all-to-all-start.1 = ((bf16[32,13,768]{2,1,0:T(8,128)(2,1)}), bf16[32,13,768]{2,1,0:T(8,128)(2,1)}, u32[]{:S(2)}, u32[]{:S(2)}) async-start(bf16[32,13,768]{2,1,0:T(8,128)(2,1)} %all_to_all.17), calls=%async_computation.1 | async-start | bytes 1572864 | tf_op jit(solution)/shard_map/all_to_all | solution.py:254
  619.7 20.6 %copy-start.32 = (f32[768]{0:T(1024)S(1)}, f32[768]{0:T(1024)}, u32[]{:S(2)}) copy-start(f32[768]{0:T(1024)} %param.42) | copy-start | bytes 9220
  619.7 24.5 %copy-start.34 = (f32[416]{0:T(512)S(1)}, f32[416]{0:T(512)}, u32[]{:S(2)}) copy-start(f32[416]{0:T(512)} %copy-done.33) | copy-start | bytes 4996
  619.7 24.5 %copy-start.38 = (f32[416]{0:T(512)S(1)}, f32[416]{0:T(512)}, u32[]{:S(2)}) copy-start(f32[416]{0:T(512)} %copy-done.37) | copy-start | bytes 4996
  619.7 559.6 %all-reduce.4.cloned.1.call-start = ((), (), s32[]{:S(2)}) async-start(), calls=%async_computation.8 | async-start | bytes 69206016 | tf_op jit(solution)/shard_map/psum | solution.py:289
  630.7 13.5 %copy-start.2 = (f32[416,768]{1,0:T(8,128)S(1)}, f32[416,768]{1,0:T(8,128)}, u32[]{:S(2)}) copy-start(f32[416,768]{1,0:T(8,128)} %copy-done.1) | copy-start | bytes 3833860
  652.0 44.7 %copy-start.40 = (bf16[4,768]{1,0:T(4,128)(2,1)S(1)}, bf16[4,768]{1,0:T(4,128)(2,1)}, u32[]{:S(2)}) copy-start(bf16[4,768]{1,0:T(4,128)(2,1)} %param.40) | copy-start | bytes 18436
  1185.8 3.4 copy-start.19
  1189.2 2.5 copy-start.18
  1191.7 2.5 copy-start.17
  1194.2 10.7 slice-start.3
  1195.6 9.3 slice-start.4
  1195.6 9.3 slice-start.5
  (21 other events, 27.7 us)
Sparse Core Ops, SparseCore 0:
  10.9 65.2 all-gather.6
  79.1 152.8 all-gather.12
  235.0 52.9 all-gather.10
  290.7 52.9 all-gather.8
  346.5 52.9 all-gather.14
  402.2 62.5 all-gather.16
  652.1 527.0 all-reduce.3
